TPU v7x, 128 devices: a whole 4x4x4 slice. The times are simulated.
128 devices in a mesh: req: 4 (over y), tile: 32 (over x, z, core).
Axes of the slice: x: 4, y: 4, z: 4, core: 2. Of those that a mesh axis runs over, the one named last changes fastest.
Arguments:
- image: bfloat16 [8, 4096, 2432], P('req', 'tile'), may hold values from -40 to 40
- text: bfloat16 [8, 154, 2432], P('req'), may hold values from -40 to 40
- pooled: float32 [8, 2432], P('req'), may hold values from -6 to 6
- timesteps: int32 [8], P('req'), may hold values from 0 to 999
- lengths: int32 [8], P('req'), may hold values from 1 to 4096, 16384 in all
- w_time: bfloat16 [256, 2432], replicated, may hold values from -0.375 to 0.375
- w_mod: bfloat16 [2432, 9728], P(None, 'tile'), may hold values from -0.125 to 0.125
- w_img: bfloat16 [2432, 6144], P(None, ('req', 'tile')), may hold values from -0.125 to 0.125
- w_txt: bfloat16 [2432, 6144], P(None, 'tile'), may hold values from -0.125 to 0.125
- q_gain: float32 [64], replicated, may hold values from 1 to 2.5
- k_gain: float32 [64], replicated, may hold values from 1 to 2.5
- text_q_gain: float32 [64], replicated, may hold values from 1 to 2.5
- text_k_gain: float32 [64], replicated, may hold values from 1 to 2.5
Outputs:
- image_attention: bfloat16 [8, 4096, 2048], P('req', 'tile')
- text_attention: bfloat16 [8, 154, 2048], P('req', None, 'tile')
Inputs may be any that keep to these rules, and one draw needn't show every extreme that they name: `lengths`: the image token counts of all 8 requests sum to 16384, and the largest is exactly 4096.
All inputs are finite; a program needn't handle non-finite values. No bound on the sum of `lengths` on one device may be relied on, other than what follows from the above.
Results may differ from a plain program's by a relative error of at most 0.02.
Values may be sent and summed in bfloat16 or wider, within the bound.
A program may use at most 128 MiB of HBM per device.

v0:
```python
import math
import jax
import jax.numpy as jnp
from jax import lax
from jax.sharding import PartitionSpec as P

epsilon = 1e-06


def time_features(step_index, feature_count):
    half_count = feature_count // 2
    frequency = jnp.exp(-math.log(10000.0) * jnp.arange(half_count, dtype=jnp.float32) / half_count)
    angles = step_index.astype(jnp.float32)[:, None] * frequency[None, :]
    return jnp.concatenate([jnp.cos(angles), jnp.sin(angles)], axis=-1).astype(jnp.bfloat16)


def modulate(tokens, shift, scale):
    values = tokens.astype(jnp.float32)
    center = jnp.mean(values, axis=-1, keepdims=True)
    spread = jnp.mean(jnp.square(values - center), axis=-1, keepdims=True)
    normed = (values - center) * lax.rsqrt(spread + epsilon)
    return (normed * (1.0 + scale.astype(jnp.float32)) + shift.astype(jnp.float32)).astype(
        jnp.bfloat16
    )


def rms_gain(vectors, gain):
    factor = lax.rsqrt(jnp.mean(jnp.square(vectors), axis=-1, keepdims=True) + epsilon)
    return (vectors * factor * gain).astype(jnp.bfloat16)


def pack_heads(qkv, head_dim, q_gain, k_gain):
    lead = qkv.shape[:2]
    head_count = qkv.shape[-1] // (3 * head_dim)
    qkv = qkv.reshape(lead + (head_count, 3, head_dim))
    return jnp.concatenate(
        [
            rms_gain(qkv[:, :, :, 0:1, :], q_gain),
            rms_gain(qkv[:, :, :, 1:2, :], k_gain),
            qkv[:, :, :, 2:3, :].astype(jnp.bfloat16),
        ],
        axis=3,
    ).reshape(lead + (head_count, 3 * head_dim))


def local(
    image,
    text,
    pooled,
    timesteps,
    lengths,
    w_time,
    w_mod,
    w_img,
    w_txt,
    q_gain,
    k_gain,
    text_q_gain,
    text_k_gain,
):
    tile_count = lax.axis_size("tile")
    group_count, local_rows, model_width = image.shape
    seq_len = local_rows * tile_count
    text_len = text.shape[1]
    head_dim = q_gain.shape[0]
    heads_here = w_txt.shape[1] // (3 * head_dim)
    score_scale = head_dim ** (-0.5)
    block = min(512, seq_len)
    features = time_features(timesteps, w_time.shape[0])
    cond_act = jax.nn.silu(
        pooled + jnp.dot(features, w_time, preferred_element_type=jnp.float32)
    ).astype(jnp.bfloat16)
    mod_part = jnp.dot(cond_act, w_mod, preferred_element_type=jnp.float32).astype(jnp.bfloat16)
    modulation = lax.all_gather(mod_part, "tile", axis=1, tiled=True)
    h_img = modulate(
        image,
        modulation[:, None, 0:model_width],
        modulation[:, None, model_width : 2 * model_width],
    )
    qkv_img = jnp.einsum(
        "gpd,dc->gpc",
        h_img,
        lax.all_gather(w_img, ("req", "tile"), axis=1, tiled=True),
        preferred_element_type=jnp.float32,
    )
    packed = pack_heads(qkv_img, head_dim, q_gain, k_gain)
    by_head = lax.all_to_all(packed, "tile", split_axis=2, concat_axis=1, tiled=True)
    by_head = by_head.reshape(group_count, seq_len, heads_here, 3, head_dim)
    h_txt = modulate(
        text,
        modulation[:, None, 2 * model_width : 3 * model_width],
        modulation[:, None, 3 * model_width : 4 * model_width],
    )
    qkv_txt = jnp.einsum("gtd,dc->gtc", h_txt, w_txt, preferred_element_type=jnp.float32).reshape(
        group_count, text_len, heads_here, 3, head_dim
    )
    text_queries = jnp.moveaxis(rms_gain(qkv_txt[:, :, :, 0, :], text_q_gain), 2, 1)
    text_keys = jnp.moveaxis(rms_gain(qkv_txt[:, :, :, 1, :], text_k_gain), 2, 1)
    text_values = jnp.moveaxis(qkv_txt[:, :, :, 2, :].astype(jnp.bfloat16), 2, 1)
    image_queries = jnp.moveaxis(by_head[:, :, :, 0, :], 2, 1)
    image_keys = jnp.moveaxis(by_head[:, :, :, 1, :], 2, 1)
    image_values = jnp.moveaxis(by_head[:, :, :, 2, :], 2, 1)
    slot_live = (jnp.arange(seq_len, dtype=jnp.int32)[None, :] < lengths[:, None]).astype(
        jnp.float32
    )
    keys = jnp.concatenate([text_keys, image_keys], axis=2)
    values = jnp.concatenate([text_values, image_values], axis=2)
    key_mask = jnp.concatenate([jnp.ones((group_count, text_len), jnp.float32), slot_live], axis=1)

    def attend_block(query_block):
        scores = (
            jnp.einsum("ghqe,ghke->ghqk", query_block, keys, preferred_element_type=jnp.float32)
            * score_scale
        )
        weights = jnp.exp(scores) * key_mask[:, None, None, :]
        total = jnp.sum(weights, axis=-1)
        summed = jnp.einsum(
            "ghqk,ghke->ghqe",
            weights.astype(jnp.bfloat16),
            values,
            preferred_element_type=jnp.float32,
        )
        return summed / total[..., None]

    text_result = attend_block(text_queries)
    block_count = seq_len // block
    query_blocks = jnp.moveaxis(
        image_queries.reshape(group_count, heads_here, block_count, block, head_dim), 2, 0
    )
    image_result = lax.map(attend_block, query_blocks)
    image_result = jnp.moveaxis(image_result, 0, 2).reshape(
        group_count, heads_here, seq_len, head_dim
    )
    image_result = image_result * slot_live[:, None, :, None]
    image_heads = (
        jnp.moveaxis(image_result, 1, 2)
        .reshape(group_count, seq_len, heads_here * head_dim)
        .astype(jnp.bfloat16)
    )
    image_attention = lax.all_to_all(image_heads, "tile", split_axis=1, concat_axis=2, tiled=True)
    text_attention = (
        jnp.moveaxis(text_result, 1, 2)
        .reshape(group_count, text_len, heads_here * head_dim)
        .astype(jnp.bfloat16)
    )
    return (image_attention, text_attention)


def solution(mesh):
    in_specs = (
        P("req", "tile", None),
        P("req", None, None),
        P("req", None),
        P("req"),
        P("req"),
        P(),
        P(None, "tile"),
        P(None, ("req", "tile")),
        P(None, "tile"),
        P(),
        P(),
        P(),
        P(),
    )
    out_specs = (P("req", "tile", None), P("req", None, "tile"))
    return jax.shard_map(local, mesh=mesh, in_specs=in_specs, out_specs=out_specs, check_vma=False)
```

profile of v0, /device:TPU:1, one launch (start us, length us, event | category | flops | bytes accessed | tf_op | source)
XLA Modules:
  0.0 318.6 jit_solution(9887825131999593207)
XLA Ops:
  10.7 26.9 %all-gather = bf16[32,304,2]{1,2,0:T(2,128)(2,1)S(1)} all-gather(bf16[1,304,2]{1,2,0:T(2,128)(2,1)S(1)} %fusion.59), channel_id=1, replica_groups=mesh['req'=4,'tile'=32] {'tile'}, dimensions={0}, use_global_device_ids=true | all-gather | bytes 40128 | tf_op jit(solution)/shard_map/all_gather | solution.py:74
  42.6 72.7 %all-gather.3.cloned.1.call-done = bf16[2432,6144]{0,1:T(8,128)(2,1)} async-done(((bf16[2432,48]{0,1:T(8,128)(2,1)}), bf16[2432,6144]{0,1:T(8,128)(2,1)}) %all-gather.3.cloned.1.call-update) | async-done | bytes 29884432 | tf_op jit(solution)/shard_map/all_gather | solution.py:83
  115.3 13.6 %fusion.26 = f32[2,128,6144]{1,2,0:T(8,128)S(1)} fusion(bf16[2432,6144]{0,1:T(8,128)(2,1)} %all-gather.3.cloned.1.call-done, bf16[2,128,2432]{2,1,0:T(8,128)(2,1)S(1)} %copy-done.3, f32[2,2432]{1,0:T(2,128)S(1)} %get-tuple-element.69, f32[2,2432]{1,0:T(2,128)S(1)} %get-tuple-element.67, f32[2,128]{1,0:T(2,128)S(1)} %add_rsqrt_fusion.5, ...), kind=kOutput, calls=%fused_computation.14 | convolution fusion | flops 7654146048 | bytes 37462016 | tf_op jit(solution)/shard_map/gpd,dc->gpc/dot_general | solution.py:80
  133.1 6.2 %all-to-all-start = ((bf16[2,128,32,192]{1,3,0,2:T(8,128)(2,1)}), bf16[2,128,32,192]{1,3,0,2:T(8,128)(2,1)}, u32[]{:S(2)}, u32[]{:S(2)}) async-start(bf16[2,128,32,192]{1,3,0,2:T(8,128)(2,1)} %copy.78), calls=%async_computation | async-start | bytes 6291456 | tf_op jit(solution)/shard_map/all_to_all | solution.py:87
  145.4 33.8 %all-to-all-done = bf16[2,128,32,192]{1,3,0,2:T(8,128)(2,1)} async-done(((bf16[2,128,32,192]{1,3,0,2:T(8,128)(2,1)}), bf16[2,128,32,192]{1,3,0,2:T(8,128)(2,1)}, u32[]{:S(2)}, u32[]{:S(2)}) %all-to-all-start) | async-done | bytes 3145760 | tf_op jit(solution)/shard_map/all_to_all | solution.py:87
  179.2 5.6 %copy.79 = bf16[2,32,128,1,192]{2,1,4,0,3:T(8,128)(2,1)} copy(bf16[2,32,128,1,192]{2,4,0,1,3:T(8,128)(2,1)} %bitcast.11) | data formatting | bytes 6291456 | tf_op jit(solution)/shard_map/all_to_all | solution.py:87
  184.8 5.8 %reshape.273 = bf16[2,4096,1,3,64]{1,4,3,0,2:T(8,128)(2,1)} reshape(bf16[2,32,128,1,192]{2,1,4,0,3:T(8,128)(2,1)} %copy.79) | data formatting | bytes 6291456 | tf_op jit(solution)/shard_map/reshape | solution.py:88
  195.3 67.5 %while.10 = (s32[]{:T(128)}, f32[8,2,1,512,64]{3,4,1,2,0:T(8,128)}, bf16[8,2,1,512,64]{3,4,1,2,0:T(8,128)(2,1)}, bf16[2,1,4250,64]{2,3,0,1:T(8,128)(2,1)S(1)}, f...) while((s32[]{:T(128)}, f32[8,2,1,512,64]{3,4,1,2,0:T(8,128)}, ...), condition=%wide.region_9.10_spmd, body=%wide.region_7.0_spmd.sunk | while | flops 1140288512 | bytes 37462508 | solution.py:130
  195.3 4.8 %fusion.93 = (f32[2,512]{1,0:T(2,128)S(1)}, f32[2,512,4250]{1,2,0:T(8,128)S(1)}) fusion(f32[2,4250]{1,0:T(2,128)S(1)} %get-tuple-element.137, bf16[2,1,4250,64]{2,3,0,1:T(8,128)(2,1)S(1)} %get-tuple-element.136, bf16[8,2,1,512,64]{3,4,1,2,0:T(8,128)(2,1)} %get-tuple-element.135, s32[]{:T(128)} %get-tuple-element.126), kind=kOutput, calls=%fused_computation.1.clone.1 | convolution fusion | flops 570110976 | bytes 18665680 | tf_op jit(solution)/shard_map/while/body/eval_jaxpr/ghqe,ghke->ghqk/dot_general | solution.py:112
  203.7 4.8 %fusion.93 = (f32[2,512]{1,0:T(2,128)S(1)}, f32[2,512,4250]{1,2,0:T(8,128)S(1)}) fusion(f32[2,4250]{1,0:T(2,128)S(1)} %get-tuple-element.137, bf16[2,1,4250,64]{2,3,0,1:T(8,128)(2,1)S(1)} %get-tuple-element.136, bf16[8,2,1,512,64]{3,4,1,2,0:T(8,128)(2,1)} %get-tuple-element.135, s32[]{:T(128)} %get-tuple-element.126), kind=kOutput, calls=%fused_computation.1.clone.1 | convolution fusion | flops 570110976 | bytes 18665680 | tf_op jit(solution)/shard_map/while/body/eval_jaxpr/ghqe,ghke->ghqk/dot_general | solution.py:112
  212.1 4.8 %fusion.93 = (f32[2,512]{1,0:T(2,128)S(1)}, f32[2,512,4250]{1,2,0:T(8,128)S(1)}) fusion(f32[2,4250]{1,0:T(2,128)S(1)} %get-tuple-element.137, bf16[2,1,4250,64]{2,3,0,1:T(8,128)(2,1)S(1)} %get-tuple-element.136, bf16[8,2,1,512,64]{3,4,1,2,0:T(8,128)(2,1)} %get-tuple-element.135, s32[]{:T(128)} %get-tuple-element.126), kind=kOutput, calls=%fused_computation.1.clone.1 | convolution fusion | flops 570110976 | bytes 18665680 | tf_op jit(solution)/shard_map/while/body/eval_jaxpr/ghqe,ghke->ghqk/dot_general | solution.py:112
  216.9 3.6 %fusion.94 = f32[8,2,1,512,64]{3,4,1,2,0:T(8,128)} fusion(f32[8,2,1,512,64]{3,4,1,2,0:T(8,128)} %get-tuple-element.127, s32[]{:T(128)} %get-tuple-element.126, bf16[2,1,4250,64]{2,3,0,1:T(8,128)(2,1)S(1)} %get-tuple-element.138, f32[2,512,4250]{1,2,0:T(8,128)S(1)} %get-tuple-element.117, f32[2,4250]{1,0:T(2,128)S(1)} %get-tuple-element.137, ...), kind=kOutput, calls=%fused_computation.9.clone.1 | convolution fusion | flops 570177536 | bytes 18796752 | tf_op jit(solution)/shard_map/while/body/eval_jaxpr/ghqk,ghke->ghqe/dot_general | solution.py:117
  220.6 4.8 %fusion.93 = (f32[2,512]{1,0:T(2,128)S(1)}, f32[2,512,4250]{1,2,0:T(8,128)S(1)}) fusion(f32[2,4250]{1,0:T(2,128)S(1)} %get-tuple-element.137, bf16[2,1,4250,64]{2,3,0,1:T(8,128)(2,1)S(1)} %get-tuple-element.136, bf16[8,2,1,512,64]{3,4,1,2,0:T(8,128)(2,1)} %get-tuple-element.135, s32[]{:T(128)} %get-tuple-element.126), kind=kOutput, calls=%fused_computation.1.clone.1 | convolution fusion | flops 570110976 | bytes 18665680 | tf_op jit(solution)/shard_map/while/body/eval_jaxpr/ghqe,ghke->ghqk/dot_general | solution.py:112
  229.0 4.8 %fusion.93 = (f32[2,512]{1,0:T(2,128)S(1)}, f32[2,512,4250]{1,2,0:T(8,128)S(1)}) fusion(f32[2,4250]{1,0:T(2,128)S(1)} %get-tuple-element.137, bf16[2,1,4250,64]{2,3,0,1:T(8,128)(2,1)S(1)} %get-tuple-element.136, bf16[8,2,1,512,64]{3,4,1,2,0:T(8,128)(2,1)} %get-tuple-element.135, s32[]{:T(128)} %get-tuple-element.126), kind=kOutput, calls=%fused_computation.1.clone.1 | convolution fusion | flops 570110976 | bytes 18665680 | tf_op jit(solution)/shard_map/while/body/eval_jaxpr/ghqe,ghke->ghqk/dot_general | solution.py:112
  237.5 4.8 %fusion.93 = (f32[2,512]{1,0:T(2,128)S(1)}, f32[2,512,4250]{1,2,0:T(8,128)S(1)}) fusion(f32[2,4250]{1,0:T(2,128)S(1)} %get-tuple-element.137, bf16[2,1,4250,64]{2,3,0,1:T(8,128)(2,1)S(1)} %get-tuple-element.136, bf16[8,2,1,512,64]{3,4,1,2,0:T(8,128)(2,1)} %get-tuple-element.135, s32[]{:T(128)} %get-tuple-element.126), kind=kOutput, calls=%fused_computation.1.clone.1 | convolution fusion | flops 570110976 | bytes 18665680 | tf_op jit(solution)/shard_map/while/body/eval_jaxpr/ghqe,ghke->ghqk/dot_general | solution.py:112
  245.9 4.8 %fusion.93 = (f32[2,512]{1,0:T(2,128)S(1)}, f32[2,512,4250]{1,2,0:T(8,128)S(1)}) fusion(f32[2,4250]{1,0:T(2,128)S(1)} %get-tuple-element.137, bf16[2,1,4250,64]{2,3,0,1:T(8,128)(2,1)S(1)} %get-tuple-element.136, bf16[8,2,1,512,64]{3,4,1,2,0:T(8,128)(2,1)} %get-tuple-element.135, s32[]{:T(128)} %get-tuple-element.126), kind=kOutput, calls=%fused_computation.1.clone.1 | convolution fusion | flops 570110976 | bytes 18665680 | tf_op jit(solution)/shard_map/while/body/eval_jaxpr/ghqe,ghke->ghqk/dot_general | solution.py:112
  250.7 3.6 %fusion.94 = f32[8,2,1,512,64]{3,4,1,2,0:T(8,128)} fusion(f32[8,2,1,512,64]{3,4,1,2,0:T(8,128)} %get-tuple-element.127, s32[]{:T(128)} %get-tuple-element.126, bf16[2,1,4250,64]{2,3,0,1:T(8,128)(2,1)S(1)} %get-tuple-element.138, f32[2,512,4250]{1,2,0:T(8,128)S(1)} %get-tuple-element.117, f32[2,4250]{1,0:T(2,128)S(1)} %get-tuple-element.137, ...), kind=kOutput, calls=%fused_computation.9.clone.1 | convolution fusion | flops 570177536 | bytes 18796752 | tf_op jit(solution)/shard_map/while/body/eval_jaxpr/ghqk,ghke->ghqe/dot_general | solution.py:117
  254.3 4.8 %fusion.93 = (f32[2,512]{1,0:T(2,128)S(1)}, f32[2,512,4250]{1,2,0:T(8,128)S(1)}) fusion(f32[2,4250]{1,0:T(2,128)S(1)} %get-tuple-element.137, bf16[2,1,4250,64]{2,3,0,1:T(8,128)(2,1)S(1)} %get-tuple-element.136, bf16[8,2,1,512,64]{3,4,1,2,0:T(8,128)(2,1)} %get-tuple-element.135, s32[]{:T(128)} %get-tuple-element.126), kind=kOutput, calls=%fused_computation.1.clone.1 | convolution fusion | flops 570110976 | bytes 18665680 | tf_op jit(solution)/shard_map/while/body/eval_jaxpr/ghqe,ghke->ghqk/dot_general | solution.py:112
  262.7 4.1 %copy.91 = f32[2,1,8,512,64]{3,2,4,0,1:T(8,128)} copy(f32[2,1,8,512,64]{3,4,0,1,2:T(8,128)} %bitcast.19) | data formatting | bytes 4194304 | tf_op jit(solution)/shard_map/transpose | solution.py:131
  271.4 3.9 %copy.92 = bf16[2,4096,64]{2,0,1:T(2,128)(2,1)} copy(bf16[2,4096,64]{1,2,0:T(8,128)(2,1)S(1)} %multiply_convert_fusion) | data formatting | bytes 2097152 | tf_op jit(solution)/shard_map/convert_element_type | solution.py:138
  275.3 5.9 %reshape.282 = bf16[32,2,8192]{2,1,0:T(2,128)(2,1)} reshape(bf16[4096,2,64]{2,1,0:T(2,128)(2,1)} %bitcast.116) | data formatting | bytes 2097152
  281.1 5.0 %all-to-all-start.1 = ((bf16[32,2,8192]{2,1,0:T(2,128)(2,1)}), bf16[32,2,8192]{2,1,0:T(2,128)(2,1)S(1)}, u32[]{:S(2)}, u32[]{:S(2)}) async-start(bf16[32,2,8192]{2,1,0:T(2,128)(2,1)} %reshape.282), calls=%async_computation.1 | async-start | bytes 2097152 | tf_op jit(solution)/shard_map/all_to_all | solution.py:140
  289.5 13.6 %all-to-all-done.1 = bf16[32,2,8192]{2,1,0:T(2,128)(2,1)S(1)} async-done(((bf16[32,2,8192]{2,1,0:T(2,128)(2,1)}), bf16[32,2,8192]{2,1,0:T(2,128)(2,1)S(1)}, u32[]{:S(2)}, u32[]{:S(2)}) %all-to-all-start.1) | async-done | bytes 1048608 | tf_op jit(solution)/shard_map/all_to_all | solution.py:140
  305.4 5.0 %copy.99 = bf16[2,32,128,64]{2,3,1,0:T(8,128)(2,1)S(1)} copy(bf16[2,32,128,64]{3,0,2,1:T(2,128)(2,1)} %bitcast.117) | data formatting | bytes 2097152 | tf_op jit(solution)/shard_map/all_to_all | solution.py:140
  (80 shorter events, 56.4 us)
Async XLA Ops:
  7.2 1.6 copy-start
  7.2 30.6 %copy-start.8 = (s32[2]{0:T(128)S(1)}, s32[2]{0:T(128)}, u32[]{:S(2)}) copy-start(s32[2]{0:T(128)} %param.19) | copy-start | bytes 28
  7.2 108.1 %all-gather.3.cloned.1.call-start = ((), (), s32[]{:S(2)}) async-start(), calls=%async_computation.2 | async-start | bytes 30117888 | tf_op jit(solution)/shard_map/all_gather | solution.py:83
  10.7 30.7 %copy-start.2 = (bf16[2,154,2432]{2,0,1:T(2,128)(2,1)S(1)}, bf16[2,154,2432]{2,0,1:T(2,128)(2,1)}, u32[]{:S(2)}) copy-start(bf16[2,154,2432]{2,0,1:T(2,128)(2,1)} %param.16) | copy-start | bytes 4494340
  37.6 77.7 %copy-start.3 = (bf16[2,128,2432]{2,1,0:T(8,128)(2,1)S(1)}, bf16[2,128,2432]{2,1,0:T(8,128)(2,1)}, u32[]{:S(2)}) copy-start(bf16[2,128,2432]{2,1,0:T(8,128)(2,1)} %param.15) | copy-start | bytes 3735556
  128.9 1.0 copy-start.10
  128.9 1.0 copy-start.11
  133.1 46.1 %all-to-all-start = ((bf16[2,128,32,192]{1,3,0,2:T(8,128)(2,1)}), bf16[2,128,32,192]{1,3,0,2:T(8,128)(2,1)}, u32[]{:S(2)}, u32[]{:S(2)}) async-start(bf16[2,128,32,192]{1,3,0,2:T(8,128)(2,1)} %copy.78), calls=%async_computation | async-start | bytes 6291456 | tf_op jit(solution)/shard_map/all_to_all | solution.py:87
  139.4 5.1 %copy-start.12 = (bf16[2432,192]{0,1:T(8,128)(2,1)S(1)}, bf16[2432,192]{0,1:T(8,128)(2,1)}, u32[]{:S(2)}) copy-start(bf16[2432,192]{0,1:T(8,128)(2,1)} %param.23) | copy-start | bytes 2801668
  144.5 0.8 copy-start.9
  192.8 2.1 copy-start.6
  192.8 2.1 copy-start.4
  275.3 10.9 %copy-start.7 = (bf16[2,1,4096,64]{2,3,0,1:T(8,128)(2,1)S(1)}, bf16[2,1,4096,64]{2,3,0,1:T(8,128)(2,1)}, u32[]{:S(2)}) copy-start(bf16[2,1,4096,64]{2,3,0,1:T(8,128)(2,1)} %copy-done.6) | copy-start | bytes 3145732
  275.3 10.9 %copy-start.13 = (f32[64]{0:T(128)S(1)}, f32[64]{0:T(128)}, u32[]{:S(2)}) copy-start(f32[64]{0:T(128)} %param.26) | copy-start | bytes 772
  281.1 21.9 %all-to-all-start.1 = ((bf16[32,2,8192]{2,1,0:T(2,128)(2,1)}), bf16[32,2,8192]{2,1,0:T(2,128)(2,1)S(1)}, u32[]{:S(2)}, u32[]{:S(2)}) async-start(bf16[32,2,8192]{2,1,0:T(2,128)(2,1)} %reshape.282), calls=%async_computation.1 | async-start | bytes 2097152 | tf_op jit(solution)/shard_map/all_to_all | solution.py:140
  286.2 1.6 copy-start.5
  305.4 6.3 %copy-start.1 = (bf16[2432,304]{0,1:T(8,128)(2,1)S(1)}, bf16[2432,304]{0,1:T(8,128)(2,1)}, u32[]{:S(2)}) copy-start(bf16[2432,304]{0,1:T(8,128)(2,1)} %param.21) | copy-start | bytes 4435972
Sparse Core Ops, SparseCore 0:
  11.0 104.2 all-gather.2
where the time goes:
time: 320 us; the launch traced here: 319 us
  waiting for transfers between devices  121 us (38%)
  matrix products  86.9 us (27%)
  local copies, waits for them, and re-layouts  43 us (13%)
  blocking collectives  26.9 us (8%)
  other arithmetic  15.2 us (5%)
  between operations  14.4 us (4%)
  starting transfers between devices  11.3 us (4%)
    all_gather x1, waiting for transfers between devices, local(): lax.all_gather(w_img, ('req', 'tile'), axis=1, tiled=True)  72.7 us
    dot_general x9, matrix products, attend_block(): jnp.einsum('ghqe,ghke->ghqk', query_block, keys, preferred_element_type=j...  39.9 us
    all_to_all x1, waiting for transfers between devices, local(): lax.all_to_all(packed, 'tile', split_axis=2, concat_axis=1, tiled=True)  33.8 us
    dot_general x9, matrix products, attend_block(): jnp.einsum('ghqk,ghke->ghqe', weights.astype(jnp.bfloat16), values, prefe...  30.8 us
    all_gather x1, blocking collectives, local(): modulation = lax.all_gather(mod_part, 'tile', axis=1, tiled=True)  26.9 us
    dot_general x1, matrix products, local(): jnp.einsum('gpd,dc->gpc', h_img, lax.all_gather(w_img, ('req', 'tile'), a...  13.6 us
    all_to_all x1, waiting for transfers between devices, local(): lax.all_to_all(image_heads, 'tile', split_axis=1, concat_axis=2, tiled=True)  13.6 us
    unnamed x33, local copies, waits for them, and re-layouts  10.1 us
  transfers between devices with their start and end apart: 3, of which 3 were waited for; matrix products, arithmetic and copies ran while one was open for 5% of the time, Pallas kernels for 0%

commit v1 on v0

--- a/solution.py
+++ b/solution.py
@@ -58,6 +58,18 @@
     text_q_gain,
     text_k_gain,
 ):
+
+    def part_the_routes_all(in_array, d0=1):
+        return jnp.concatenate(
+            lax.all_to_all(
+                jnp.stack([in_array] * lax.psum(1, axis_name=("req", "tile")), axis=0),
+                concat_axis=0,
+                axis_name=("req", "tile"),
+                split_axis=0,
+            ),
+            axis=d0,
+        )
+
     tile_count = lax.axis_size("tile")
     group_count, local_rows, model_width = image.shape
     seq_len = local_rows * tile_count
@@ -78,10 +90,7 @@
         modulation[:, None, model_width : 2 * model_width],
     )
     qkv_img = jnp.einsum(
-        "gpd,dc->gpc",
-        h_img,
-        lax.all_gather(w_img, ("req", "tile"), axis=1, tiled=True),
-        preferred_element_type=jnp.float32,
+        "gpd,dc->gpc", h_img, part_the_routes_all(w_img), preferred_element_type=jnp.float32
     )
     packed = pack_heads(qkv_img, head_dim, q_gain, k_gain)
     by_head = lax.all_to_all(packed, "tile", split_axis=2, concat_axis=1, tiled=True)

time: 320 us -> 694 us (2.17)
  blocking collectives: 26.9 us -> 463 us
  waiting for transfers between devices: 121 us -> 47.3 us
  between operations: 14.4 us -> 1.07 us
  local copies, waits for them, and re-layouts: 43 us -> 53.9 us
  starting transfers between devices: 11.3 us -> 21.6 us
    all_gather x1, blocking collectives: 26.9 us -> 463 us  [local(): modulation = lax.all_gather(mod_part, 'tile', axis=1, tiled=True)]
    all_gather x1 -> x0, waiting for transfers between devices: 72.7 us -> none  [local(): lax.all_gather(w_img, ('req', 'tile'), axis=1, tiled=True)]
    all_to_all x0 -> x1, starting transfers between devices: none -> 11.9 us  [part_the_routes_all(): lax.all_to_all(jnp.stack([in_array] * lax.psum(1, axis_name=('req', 'tile...]
    another operation x0 -> x1, local copies, waits for them, and re-layouts: none -> 10.9 us  [part_the_routes_all(): jnp.stack([in_array] * lax.psum(1, axis_name=('req', 'tile')), axis=0)]
  transfers between devices with their start and end apart: 3 -> 3, of which waited for: 3 -> 2; matrix products, arithmetic and copies ran while one was open for 5% -> 2% of each run, Pallas kernels for 0% -> 0%
where the time goes in v1:
time: 694 us; the launch traced here: 690 us
  blocking collectives  463 us (67%)
  matrix products  89.6 us (13%)
  local copies, waits for them, and re-layouts  53.9 us (8%)
  waiting for transfers between devices  47.3 us (7%)
  starting transfers between devices  21.6 us (3%)
  other arithmetic  13.2 us (2%)
    all_gather x1, blocking collectives, local(): modulation = lax.all_gather(mod_part, 'tile', axis=1, tiled=True)  463 us
    dot_general x9, matrix products, attend_block(): jnp.einsum('ghqe,ghke->ghqk', query_block, keys, preferred_element_type=j...  40 us
    all_to_all x1, waiting for transfers between devices, local(): lax.all_to_all(packed, 'tile', split_axis=2, concat_axis=1, tiled=True)  33.7 us
    dot_general x9, matrix products, attend_block(): jnp.einsum('ghqk,ghke->ghqe', weights.astype(jnp.bfloat16), values, prefe...  30.7 us
    dot_general x1, matrix products, local(): jnp.einsum('gpd,dc->gpc', h_img, part_the_routes_all(w_img), preferred_el...  16.2 us
  transfers between devices with their start and end apart: 3, of which 2 were waited for; matrix products, arithmetic and copies ran while one was open for 2% of the time, Pallas kernels for 0%

profile of v1, /device:TPU:1, one launch (start us, length us, event | category | flops | bytes accessed | tf_op | source)
XLA Modules:
  0.0 690.0 jit_solution(4450447239714247921)
XLA Ops:
  0.6 10.9 %stack.2 = bf16[128,2432,48]{1,2,0:T(8,128)(2,1)} broadcast(bf16[2432,48]{0,1:T(8,128)(2,1)} %param.22), dimensions={1,2} | broadcast | bytes 30117888 | tf_op jit(solution)/shard_map/stack | solution.py:65
  11.5 11.9 %all-to-all-start = ((bf16[128,2432,48]{1,2,0:T(8,128)(2,1)}), bf16[128,2432,48]{1,2,0:T(8,128)(2,1)}, u32[]{:S(2)}, u32[]{:S(2)}) async-start(bf16[128,2432,48]{1,2,0:T(8,128)(2,1)} %stack.2), calls=%async_computation | async-start | bytes 59768832 | tf_op jit(solution)/shard_map/all_to_all | solution.py:64
  25.7 463.3 %all-gather = bf16[32,304,2]{1,2,0:T(2,128)(2,1)S(1)} all-gather(bf16[1,304,2]{1,2,0:T(2,128)(2,1)S(1)} %fusion.59), channel_id=1, replica_groups=mesh['req'=4,'tile'=32] {'tile'}, dimensions={0}, use_global_device_ids=true | all-gather | bytes 40128 | tf_op jit(solution)/shard_map/all_gather | solution.py:86
  492.7 16.2 %fusion.45 = f32[2,128,32,3,64]{1,4,3,2,0:T(8,128)S(1)} fusion(bf16[32,3,64,2432,1]{3,2,1,0,4:T(8,128)(2,1)} %bitcast.13, bf16[2,128,2432]{2,1,0:T(8,128)(2,1)S(1)} %copy-done.3, f32[2,2432]{1,0:T(2,128)S(1)} %get-tuple-element.69, f32[2,2432]{1,0:T(2,128)S(1)} %get-tuple-element.67, f32[2,128]{1,0:T(2,128)S(1)} %add_rsqrt_fusion.5, ...), kind=kOutput, calls=%fused_computation.46 | convolution fusion | flops 7654146048 | bytes 37462016 | tf_op jit(solution)/shard_map/gpd,dc->gpc/dot_general | solution.py:92
  513.1 4.8 all-to-all-start.1
  523.9 33.7 %all-to-all-done.1 = bf16[2,128,32,192]{1,3,0,2:T(8,128)(2,1)} async-done(((bf16[2,128,32,192]{1,3,0,2:T(8,128)(2,1)}), bf16[2,128,32,192]{1,3,0,2:T(8,128)(2,1)}, u32[]{:S(2)}, u32[]{:S(2)}) %all-to-all-start.1) | async-done | bytes 3145760 | tf_op jit(solution)/shard_map/all_to_all | solution.py:96
  557.6 5.6 copy.75
  563.2 5.8 reshape.281
  573.7 67.4 %while.10 = (s32[]{:T(128)}, f32[8,2,1,512,64]{3,4,1,2,0:T(8,128)}, bf16[8,2,1,512,64]{3,4,1,2,0:T(8,128)(2,1)}, bf16[2,1,4250,64]{2,3,0,1:T(8,128)(2,1)S(1)}, f...) while((s32[]{:T(128)}, f32[8,2,1,512,64]{3,4,1,2,0:T(8,128)}, ...), condition=%wide.region_9.10_spmd, body=%wide.region_7.0_spmd.sunk | while | flops 1140288512 | bytes 37462508 | solution.py:139
  573.7 4.8 fusion.94
  582.2 4.8 fusion.94
  590.6 4.8 fusion.94
  599.0 4.8 fusion.94
  607.4 4.8 fusion.94
  615.9 4.8 fusion.94
  624.3 4.8 fusion.94
  629.1 3.6 fusion.95
  632.7 4.8 fusion.94
  641.1 4.1 copy.87
  649.8 3.9 copy.88
  653.7 5.9 reshape.291
  659.5 4.9 all-to-all-start.2
  667.8 13.6 %all-to-all-done.2 = bf16[32,2,8192]{2,1,0:T(2,128)(2,1)S(1)} async-done(((bf16[32,2,8192]{2,1,0:T(2,128)(2,1)}), bf16[32,2,8192]{2,1,0:T(2,128)(2,1)S(1)}, u32[]{:S(2)}, u32[]{:S(2)}) %all-to-all-start.2) | async-done | bytes 1048608 | tf_op jit(solution)/shard_map/all_to_all | solution.py:149
  683.7 5.0 copy.95
  (84 shorter events, 57.4 us)
Async XLA Ops:
  0.6 23.0 %copy-start = (bf16[2432,304]{0,1:T(8,128)(2,1)S(1)}, bf16[2432,304]{0,1:T(8,128)(2,1)}, u32[]{:S(2)}) copy-start(bf16[2432,304]{0,1:T(8,128)(2,1)} %param.21) | copy-start | bytes 4435972
  11.5 11.9 %copy-start.14 = (s32[2]{0:T(128)S(1)}, s32[2]{0:T(128)}, u32[]{:S(2)}) copy-start(s32[2]{0:T(128)} %param.18) | copy-start | bytes 28
  11.5 12.1 %copy-start.8 = (f32[2,2432]{1,0:T(2,128)S(1)}, f32[2,2432]{1,0:T(2,128)}, u32[]{:S(2)}) copy-start(f32[2,2432]{1,0:T(2,128)} %param.17) | copy-start | bytes 58372
  11.5 481.2 %all-to-all-start = ((bf16[128,2432,48]{1,2,0:T(8,128)(2,1)}), bf16[128,2432,48]{1,2,0:T(8,128)(2,1)}, u32[]{:S(2)}, u32[]{:S(2)}) async-start(bf16[128,2432,48]{1,2,0:T(8,128)(2,1)} %stack.2), calls=%async_computation | async-start | bytes 59768832 | tf_op jit(solution)/shard_map/all_to_all | solution.py:64
  23.4 465.7 %copy-start.9 = (s32[2]{0:T(128)S(1)}, s32[2]{0:T(128)}, u32[]{:S(2)}) copy-start(s32[2]{0:T(128)} %param.19) | copy-start | bytes 28
  23.6 467.8 %copy-start.2 = (bf16[2,154,2432]{2,0,1:T(2,128)(2,1)S(1)}, bf16[2,154,2432]{2,0,1:T(2,128)(2,1)}, u32[]{:S(2)}) copy-start(bf16[2,154,2432]{2,0,1:T(2,128)(2,1)} %param.16) | copy-start | bytes 4494340
  25.7 465.2 %copy-start.3 = (bf16[2,128,2432]{2,1,0:T(8,128)(2,1)S(1)}, bf16[2,128,2432]{2,1,0:T(8,128)(2,1)}, u32[]{:S(2)}) copy-start(bf16[2,128,2432]{2,1,0:T(8,128)(2,1)} %param.15) | copy-start | bytes 3735556
  508.9 1.0 copy-start.11
  508.9 1.0 copy-start.12
  513.1 44.5 %all-to-all-start.1 = ((bf16[2,128,32,192]{1,3,0,2:T(8,128)(2,1)}), bf16[2,128,32,192]{1,3,0,2:T(8,128)(2,1)}, u32[]{:S(2)}, u32[]{:S(2)}) async-start(bf16[2,128,32,192]{1,3,0,2:T(8,128)(2,1)} %copy.74), calls=%async_computation.1 | async-start | bytes 6291456 | tf_op jit(solution)/shard_map/all_to_all | solution.py:96
  517.9 5.1 copy-start.13
  523.1 0.8 copy-start.10
  571.2 2.1 copy-start.6
  571.2 2.1 copy-start.4
  653.7 10.8 %copy-start.7 = (bf16[2,1,4096,64]{2,3,0,1:T(8,128)(2,1)S(1)}, bf16[2,1,4096,64]{2,3,0,1:T(8,128)(2,1)}, u32[]{:S(2)}) copy-start(bf16[2,1,4096,64]{2,3,0,1:T(8,128)(2,1)} %copy-done.6) | copy-start | bytes 3145732
  653.7 10.8 %copy-start.15 = (f32[64]{0:T(128)S(1)}, f32[64]{0:T(128)}, u32[]{:S(2)}) copy-start(f32[64]{0:T(128)} %param.26) | copy-start | bytes 772
  659.5 21.8 %all-to-all-start.2 = ((bf16[32,2,8192]{2,1,0:T(2,128)(2,1)}), bf16[32,2,8192]{2,1,0:T(2,128)(2,1)S(1)}, u32[]{:S(2)}, u32[]{:S(2)}) async-start(bf16[32,2,8192]{2,1,0:T(2,128)(2,1)} %reshape.291), calls=%async_computation.2 | async-start | bytes 2097152 | tf_op jit(solution)/shard_map/all_to_all | solution.py:149
  664.5 1.6 copy-start.5
  683.7 6.3 copy-start.1
